TPU v7x, 256 devices: a whole 4x4x8 slice. The times are simulated.
256 devices in a mesh: sy: 16 (over x, y_hi, core), sx: 16 (over y_lo, z).
Axes of the slice: x: 4, y: 4 (y_hi: 2, y_lo: 2; y = y_hi * 2 + y_lo), z: 8, core: 2. Of those that a mesh axis runs over, the one named last changes fastest.
Arguments:
- object_tile: float32 [2, 2048, 2048], P(None, 'sy', 'sx'), may hold values from -5 to 5
- probe_modes: float32 [2, 2, 128, 128], replicated, may hold values from -4 to 4
- scan_offsets: int32 [16, 16, 4, 2], P('sy', 'sx'), may hold values from 0 to 128
- intensities: float32 [16, 16, 4, 128, 128], P('sy', 'sx'), may hold values from 0 to 2
Outputs:
- object_out: float32 [2, 2048, 2048], P(None, 'sy', 'sx')
- probe_out: float32 [2, 2, 128, 128], replicated
Inputs may be any that keep to these rules, and one draw needn't show every extreme that they name: `scan_offsets`: offsets are counted from 64 pixels above and to the left of the device's tile, so a patch stays within 64 pixels of its tile.
All inputs are finite; a program needn't handle non-finite values.
Results may differ from a plain program's by a relative error of at most 0.0003.
Values sent between devices are 32-bit elements; how exact they have to be, the bound alone decides.
A program may use at most 64 MiB of HBM per device.

v0:
```python
import jax
import jax.numpy as jnp
from jax import lax
from jax.sharding import PartitionSpec as P

ITERS = 2
HIGHEST = lax.Precision.HIGHEST
OBJECT_STEP = 0.5
PROBE_STEP = 2.0
REGULAR = 1.0


def extended(block, sides, width):
    for axis, dim in sides:
        count = lax.axis_size(axis)
        forward = [(i, i + 1) for i in range(count - 1)]
        backward = [(target, source) for source, target in forward]
        low = lax.ppermute(
            lax.slice_in_dim(block, block.shape[dim] - width, None, axis=dim), axis, forward
        )
        high = lax.ppermute(lax.slice_in_dim(block, 0, width, axis=dim), axis, backward)
        block = jnp.concatenate([low, block, high], axis=dim)
    return block


def shifted(value, axis, steps):
    count = lax.axis_size(axis)
    first, last = (max(0, -steps), min(count, count - steps))
    return lax.ppermute(value, axis, [(source, source + steps) for source in range(first, last)])


def tables(extent):
    index_line = jnp.arange(extent, dtype=jnp.int32)
    phase = index_line[:, None] * index_line[None, :] % extent
    angle = phase.astype(jnp.float32) * (2.0 * jnp.pi / extent)
    scale = 1.0 / jnp.sqrt(jnp.float32(extent))
    return (jnp.cos(angle) * scale, jnp.sin(angle) * scale)


def apply_left(matrix, values):
    return jnp.einsum("ux,bxy->buy", matrix, values, precision=HIGHEST)


def apply_right(values, matrix):
    return jnp.einsum("bxy,yv->bxv", values, matrix, precision=HIGHEST)


def transform(real_part, imag_part, cosine_table, sine_table, direction):
    half_real = apply_left(cosine_table, real_part) + direction * apply_left(sine_table, imag_part)
    half_imag = apply_left(cosine_table, imag_part) - direction * apply_left(sine_table, real_part)
    out_real = apply_right(half_real, cosine_table) + direction * apply_right(half_imag, sine_table)
    out_imag = apply_right(half_imag, cosine_table) - direction * apply_right(half_real, sine_table)
    return (out_real, out_imag)


def local_terms(canvas, probe_modes, offsets, measured):
    extent = probe_modes.shape[-1]
    mode_count = probe_modes.shape[0]
    positions = offsets.shape[0]
    patches = jax.vmap(
        lambda corner: lax.dynamic_slice(
            canvas, (jnp.int32(0), corner[0], corner[1]), (2, extent, extent)
        )
    )(offsets)
    object_real = patches[:, 0][:, None]
    object_imag = patches[:, 1][:, None]
    probe_real = probe_modes[:, 0][None]
    probe_imag = probe_modes[:, 1][None]
    exit_real = (probe_real * object_real - probe_imag * object_imag).reshape(
        positions * mode_count, extent, extent
    )
    exit_imag = (probe_real * object_imag + probe_imag * object_real).reshape(
        positions * mode_count, extent, extent
    )
    cosine_table, sine_table = tables(extent)
    spectrum_real, spectrum_imag = transform(exit_real, exit_imag, cosine_table, sine_table, 1.0)
    spectrum_real = spectrum_real.reshape(positions, mode_count, extent, extent)
    spectrum_imag = spectrum_imag.reshape(positions, mode_count, extent, extent)
    misfit = (
        jnp.sum(spectrum_real * spectrum_real + spectrum_imag * spectrum_imag, axis=1) - measured
    )
    back_real, back_imag = transform(
        (misfit[:, None] * spectrum_real).reshape(-1, extent, extent),
        (misfit[:, None] * spectrum_imag).reshape(-1, extent, extent),
        cosine_table,
        sine_table,
        -1.0,
    )
    back_real = back_real.reshape(positions, mode_count, extent, extent)
    back_imag = back_imag.reshape(positions, mode_count, extent, extent)
    grad_real = jnp.sum(probe_real * back_real + probe_imag * back_imag, axis=1)
    grad_imag = jnp.sum(probe_real * back_imag - probe_imag * back_real, axis=1)
    lighting = jnp.broadcast_to(
        jnp.sum(probe_real * probe_real + probe_imag * probe_imag, axis=1), grad_real.shape
    )
    terms = jnp.stack([grad_real, grad_imag, lighting], axis=1)
    numer_real = jnp.sum(object_real * back_real + object_imag * back_imag, axis=0)
    numer_imag = jnp.sum(object_real * back_imag - object_imag * back_real, axis=0)
    numerator = jnp.stack([numer_real, numer_imag], axis=1)
    denominator = jnp.sum(
        object_real[:, 0] * object_real[:, 0] + object_imag[:, 0] * object_imag[:, 0], axis=0
    )

    def place_patch(number, running):
        corner = offsets[number]
        existing = lax.dynamic_slice(
            running, (jnp.int32(0), corner[0], corner[1]), (3, extent, extent)
        )
        return lax.dynamic_update_slice(
            running, existing + terms[number], (jnp.int32(0), corner[0], corner[1])
        )

    gradients = lax.fori_loop(
        0, positions, place_patch, jnp.zeros((3,) + canvas.shape[1:], jnp.float32)
    )
    return (gradients, numerator, denominator)


def probe_update(probe_modes, numerator, denominator):
    extent = probe_modes.shape[-1]
    flat_numer = numerator.reshape(-1, extent * extent)
    flat_denom = denominator.reshape(extent * extent)
    flat_probe = probe_modes.reshape(-1, extent * extent)
    total_numer, total_denom = lax.psum((flat_numer, flat_denom), ("sy", "sx"))
    updated = flat_probe - PROBE_STEP * total_numer / (total_denom[None] + REGULAR)
    return updated.reshape(probe_modes.shape)


def fetch(current, halo_width):
    return extended(current, (("sy", 1), ("sx", 2)), halo_width)


def owner_sum(gradients, tile_size, halo_width):
    upper_rim = gradients[:, :halo_width]
    lower_rim = gradients[:, halo_width + tile_size :]
    from_above = shifted(lower_rim, "sy", 1)
    from_below = shifted(upper_rim, "sy", -1)
    middle = gradients[:, halo_width : halo_width + tile_size]
    middle = (
        middle.at[:, :halo_width].add(from_above).at[:, tile_size - halo_width :].add(from_below)
    )
    left_rim = middle[:, :, :halo_width]
    right_rim = middle[:, :, halo_width + tile_size :]
    from_left = shifted(right_rim, "sx", 1)
    from_right = shifted(left_rim, "sx", -1)
    owned = middle[:, :, halo_width : halo_width + tile_size]
    return (
        owned.at[:, :, :halo_width]
        .add(from_left)
        .at[:, :, tile_size - halo_width :]
        .add(from_right)
    )


def per_device(object_tile, probe_modes, scan_offsets, intensities):
    tile_size = object_tile.shape[1]
    halo_width = probe_modes.shape[-1] // 2
    offsets = scan_offsets[0, 0]
    measured = intensities[0, 0]
    current = object_tile
    for iteration in range(ITERS):
        canvas = fetch(current, halo_width)
        gradients, numerator, denominator = local_terms(canvas, probe_modes, offsets, measured)
        owned = owner_sum(gradients, tile_size, halo_width)
        fresh_probe = probe_update(probe_modes, numerator, denominator)
        current = current - OBJECT_STEP * owned[:2] / (owned[2:3] + REGULAR)
        probe_modes = fresh_probe
    return (current, probe_modes)


def solution(mesh):
    placed = (P(None, "sy", "sx"), P(), P("sy", "sx", None, None), P("sy", "sx", None, None, None))
    return jax.shard_map(
        per_device,
        mesh=mesh,
        in_specs=placed,
        out_specs=(P(None, "sy", "sx"), P()),
        check_vma=False,
    )
```

profile of v0, /device:TPU:8, one launch (start us, length us, event | category | flops | bytes accessed | tf_op | source)
XLA Modules:
  0.0 710.8 jit_solution(12127745365018270601)
XLA Ops:
  11.5 3.7 collective-permute-done.1
  15.4 3.8 collective-permute-start.2
  19.2 6.6 collective-permute-start.3
  30.1 8.2 %while.38 = (s32[]{:T(128)}, f32[2,256,256]{2,1,0:T(8,128)S(1)}, s32[4,3]{1,0:T(4,128)S(1)}, f32[4,2,128,128]{3,2,1,0:T(8,128)S(1)}, s32[]{:T(128)}) while((s32[]{:T(128)}, f32[2,256,256]{2,1,0:T(8,128)S(1)}, s32[4,3]{1,0:T(4,128)S(1)}, f32[4,2,128,128]{3,2,1,0:T(8,128)S(1)}, s32[]{:T(128)}) %tuple.147), condition=%wide.while_cond.8, body=%wide.while_body.8.sunk | while | flops 2 | bytes 262261 | solution.py:61
  58.7 29.5 %while.36 = (s32[]{:T(128)}, f32[3,256,256]{2,1,0:T(8,128)S(1)}, s32[4,2]{0,1:T(2,128)S(1)}, f32[4,3,128,128]{3,2,1,0:T(8,128)S(1)}, s32[]{:T(128)}, /*index=5*/s32[]{:T(128)}, s32[]{:T(128)}) while((s32[]{:T(128)}, f32[3,256,256]{2,1,0:T(8,128)S(1)}, s32[4,2]{0,1:T(2,128)S(1)}, f32[4,3,128,128]{3,2,1,0:T(8,128)S(1)}, s32[]{:T(128)}, ...), condition=%wide.region_5.6_spmd, body=%wide.region_4.5_spmd.sunk | while | flops 49160 | bytes 983237 | solution.py:113
  63.2 2.9 dynamic_update_slice.16
  70.7 2.8 dynamic_update_slice.16
  78.0 2.8 dynamic_update_slice.16
  85.4 2.8 dynamic_update_slice.16
  88.9 6.5 collective-permute-start.4
  102.6 246.5 %all-reduce.7.cloned.1.call-done = (f32[4,16384]{1,0:T(4,128)}, f32[16384]{0:T(1024)}) async-done(((f32[4,16384]{1,0:T(4,128)}, f32[16384]{0:T(1024)}), (f32[4,16384]{1,0:T(4,128)}, f32[16384]{0:T(1024)})) %all-reduce.7.cloned.1.call-update) | async-done | bytes 327696 | tf_op jit(solution)/shard_map/psum | solution.py:124
  352.6 6.3 collective-permute-done.7
  364.0 3.6 collective-permute-done.9
  370.3 5.4 collective-permute-start.11
  379.9 8.3 %while.39 = (s32[]{:T(128)}, f32[2,256,256]{2,1,0:T(8,128)S(1)}, s32[4,3]{1,0:T(4,128)S(1)}, f32[4,2,128,128]{3,2,1,0:T(8,128)S(1)}, s32[]{:T(128)}) while((s32[]{:T(128)}, f32[2,256,256]{2,1,0:T(8,128)S(1)}, s32[4,3]{1,0:T(4,128)S(1)}, f32[4,2,128,128]{3,2,1,0:T(8,128)S(1)}, s32[]{:T(128)}) %tuple.167), condition=%wide.while_cond.9, body=%wide.while_body.9.sunk | while | flops 2 | bytes 262261 | solution.py:61
  408.8 29.5 %while.37 = (s32[]{:T(128)}, f32[3,256,256]{2,1,0:T(8,128)S(1)}, s32[4,2]{0,1:T(2,128)S(1)}, f32[4,3,128,128]{3,2,1,0:T(8,128)S(1)}, s32[]{:T(128)}, /*index=5*/s32[]{:T(128)}, s32[]{:T(128)}) while((s32[]{:T(128)}, f32[3,256,256]{2,1,0:T(8,128)S(1)}, s32[4,2]{0,1:T(2,128)S(1)}, f32[4,3,128,128]{3,2,1,0:T(8,128)S(1)}, s32[]{:T(128)}, ...), condition=%wide.region_16.17_spmd, body=%wide.region_15.16_spmd.sunk | while | flops 49160 | bytes 983237 | solution.py:113
  413.4 2.9 dynamic_update_slice.17
  420.9 2.8 dynamic_update_slice.17
  428.2 2.8 dynamic_update_slice.17
  435.6 2.8 dynamic_update_slice.17
  438.5 5.4 collective-permute-start.12
  445.2 242.4 %all-reduce.5.cloned.1.call-done = (f32[4,16384]{1,0:T(4,128)}, f32[16384]{0:T(1024)}) async-done(((f32[4,16384]{1,0:T(4,128)}, f32[16384]{0:T(1024)}), (f32[4,16384]{1,0:T(4,128)}, f32[16384]{0:T(1024)})) %all-reduce.5.cloned.1.call-update) | async-done | bytes 327696 | tf_op jit(solution)/shard_map/psum | solution.py:124
  688.6 3.2 collective-permute-start.14
  692.8 4.7 collective-permute-start.15
  (203 shorter events, 103.7 us)
Async XLA Ops:
  7.2 341.9 %all-reduce.7.cloned.1.call-start = ((), (), s32[]{:S(2)}) async-start(), calls=%async_computation.1 | async-start | bytes 655360 | tf_op jit(solution)/shard_map/psum | solution.py:124
  7.2 4.1 copy-start.11
  8.1 3.4 copy-start.3
  8.1 3.3 collective-permute-start
  10.0 5.2 collective-permute-start.1
  15.2 10.6 %copy-start.7 = (f32[2,2,128,128]{3,2,1,0:T(8,128)S(1)}, f32[2,2,128,128]{3,2,1,0:T(8,128)}, u32[]{:S(2)}) copy-start(f32[2,2,128,128]{3,2,1,0:T(8,128)} %param.25) | copy-start | bytes 786436
  15.4 12.9 %collective-permute-start.2 = (f32[2,256,64]{2,1,0:T(8,128)S(1)}, f32[2,256,64]{2,1,0:T(8,128)S(1)}, u32[]{:S(2)}, u32[]{:S(2)}) collective-permute-start(f32[2,256,64]{2,1,0:T(8,128)S(1)} %get-tuple-element.354), channel_id=1, source_target_pairs={{0,1},{1,2},{2,3},{3,4},{4,5},{5,6},{6,7},{7,8},{8,9},{9,10},{10,1... | collective-permute-start | bytes 393224 | tf_op jit(solution)/shard_map/ppermute | solution.py:18
  19.2 10.5 %collective-permute-start.3 = (f32[2,256,64]{2,1,0:T(8,128)S(1)}, f32[2,256,64]{2,1,0:T(8,128)S(1)}, u32[]{:S(2)}, u32[]{:S(2)}) collective-permute-start(f32[2,256,64]{2,1,0:T(8,128)S(1)} %get-tuple-element.355), channel_id=1, source_target_pairs={{1,0},{2,1},{3,2},{4,3},{5,4},{6,5},{7,6},{8,7},{9,8},{10,9},{11,1... | collective-permute-start | bytes 393224 | tf_op jit(solution)/shard_map/ppermute | solution.py:21
  88.9 7.8 %copy-start.1 = (f32[4,128,128]{2,1,0:T(8,128)S(1)}, f32[4,128,128]{2,1,0:T(8,128)}, u32[]{:S(2)}) copy-start(f32[4,128,128]{2,1,0:T(8,128)} %copy-done) | copy-start | bytes 786436
  88.9 7.8 %copy-start.2 = (f32[8,128,128]{2,1,0:T(8,128)S(1)}, f32[8,128,128]{2,1,0:T(8,128)}, u32[]{:S(2)}) copy-start(f32[8,128,128]{2,1,0:T(8,128)} %get-tuple-element.367) | copy-start | bytes 1572868
  88.9 9.6 %collective-permute-start.4 = (f32[3,64,256]{2,1,0:T(8,128)}, f32[3,64,256]{2,1,0:T(8,128)}, u32[]{:S(2)}, u32[]{:S(2)}) collective-permute-start(f32[3,64,256]{2,1,0:T(8,128)} %get-tuple-element.339), channel_id=1, source_target_pairs={{0,16},{16,32},{32,48},{48,64},{64,80},{80,96},{96,112},{112,128},... | collective-permute-start | bytes 589832 | tf_op jit(solution)/shard_map/ppermute | solution.py:29
  95.4 4.1 collective-permute-start.5
  98.5 589.0 %all-reduce.5.cloned.1.call-start = ((), (), s32[]{:S(2)}) async-start(), calls=%async_computation | async-start | bytes 655360 | tf_op jit(solution)/shard_map/psum | solution.py:124
  100.6 251.3 %collective-permute-start.6 = (f32[3,128,64]{2,1,0:T(8,128)S(1)}, f32[3,128,64]{2,1,0:T(8,128)S(1)}, u32[]{:S(2)}, u32[]{:S(2)}) collective-permute-start(f32[3,128,64]{2,1,0:T(8,128)S(1)} %get-tuple-element.345), channel_id=1, source_target_pairs={{0,1},{1,2},{2,3},{3,4},{4,5},{5,6},{6,7},{7,8},{8,9},{9,10},{10,1... | collective-permute-start | bytes 294920 | tf_op jit(solution)/shard_map/ppermute | solution.py:29
  350.0 8.8 %collective-permute-start.7 = (f32[3,128,64]{2,1,0:T(8,128)S(1)}, f32[3,128,64]{2,1,0:T(8,128)S(1)}, u32[]{:S(2)}, u32[]{:S(2)}) collective-permute-start(f32[3,128,64]{2,1,0:T(8,128)S(1)} %get-tuple-element.344), channel_id=1, source_target_pairs={{1,0},{2,1},{3,2},{4,3},{5,4},{6,5},{7,6},{8,7},{9,8},{10,9},{11,1... | collective-permute-start | bytes 294920 | tf_op jit(solution)/shard_map/ppermute | solution.py:29
  361.0 3.0 collective-permute-start.8
  362.4 5.2 collective-permute-start.9
  367.8 10.4 %collective-permute-start.10 = (f32[2,256,64]{2,1,0:T(8,128)S(1)}, f32[2,256,64]{2,1,0:T(8,128)S(1)}, u32[]{:S(2)}, u32[]{:S(2)}) collective-permute-start(f32[2,256,64]{2,1,0:T(8,128)S(1)} %get-tuple-element.348), channel_id=1, source_target_pairs={{0,1},{1,2},{2,3},{3,4},{4,5},{5,6},{6,7},{7,8},{8,9},{9,10},{10,1... | collective-permute-start | bytes 393224 | tf_op jit(solution)/shard_map/ppermute | solution.py:18
  370.3 9.3 %collective-permute-start.11 = (f32[2,256,64]{2,1,0:T(8,128)S(1)}, f32[2,256,64]{2,1,0:T(8,128)S(1)}, u32[]{:S(2)}, u32[]{:S(2)}) collective-permute-start(f32[2,256,64]{2,1,0:T(8,128)S(1)} %get-tuple-element.349), channel_id=1, source_target_pairs={{1,0},{2,1},{3,2},{4,3},{5,4},{6,5},{7,6},{8,7},{9,8},{10,9},{11,1... | collective-permute-start | bytes 393224 | tf_op jit(solution)/shard_map/ppermute | solution.py:21
  438.5 249.9 %collective-permute-start.12 = (f32[3,64,256]{2,1,0:T(8,128)S(1)}, f32[3,64,256]{2,1,0:T(8,128)S(1)}, u32[]{:S(2)}, u32[]{:S(2)}) collective-permute-start(f32[3,64,256]{2,1,0:T(8,128)S(1)} %get-tuple-element.335), channel_id=1, source_target_pairs={{0,16},{16,32},{32,48},{48,64},{64,80},{80,96},{96,112},{112,128},... | collective-permute-start | bytes 589832 | tf_op jit(solution)/shard_map/ppermute | solution.py:29
  443.9 244.5 %collective-permute-start.13 = (f32[3,64,256]{2,1,0:T(8,128)S(1)}, f32[3,64,256]{2,1,0:T(8,128)S(1)}, u32[]{:S(2)}, u32[]{:S(2)}) collective-permute-start(f32[3,64,256]{2,1,0:T(8,128)S(1)} %get-tuple-element.334), channel_id=1, source_target_pairs={{16,0},{32,16},{48,32},{64,48},{80,64},{96,80},{112,96},{128,112},... | collective-permute-start | bytes 589832 | tf_op jit(solution)/shard_map/ppermute | solution.py:29
  688.5 3.4 copy-start.10
  688.6 10.9 %collective-permute-start.14 = (f32[3,128,64]{2,1,0:T(8,128)S(1)}, f32[3,128,64]{2,1,0:T(8,128)S(1)}, u32[]{:S(2)}, u32[]{:S(2)}) collective-permute-start(f32[3,128,64]{2,1,0:T(8,128)S(1)} %get-tuple-element.343), channel_id=1, source_target_pairs={{0,1},{1,2},{2,3},{3,4},{4,5},{5,6},{6,7},{7,8},{8,9},{9,10},{10,1... | collective-permute-start | bytes 294920 | tf_op jit(solution)/shard_map/ppermute | solution.py:29
  692.8 8.9 %collective-permute-start.15 = (f32[3,128,64]{2,1,0:T(8,128)S(1)}, f32[3,128,64]{2,1,0:T(8,128)S(1)}, u32[]{:S(2)}, u32[]{:S(2)}) collective-permute-start(f32[3,128,64]{2,1,0:T(8,128)S(1)} %get-tuple-element.342), channel_id=1, source_target_pairs={{1,0},{2,1},{3,2},{4,3},{5,4},{6,5},{7,6},{8,7},{9,8},{10,9},{11,1... | collective-permute-start | bytes 294920 | tf_op jit(solution)/shard_map/ppermute | solution.py:29
  (6 other events, 9.5 us)
Sparse Core Ops, SparseCore 0:
  98.6 250.3 all-reduce.6
  438.6 248.9 all-reduce.4
where the time goes:
time: 721 us; the launch traced here: 711 us
  waiting for transfers between devices  514 us (71%)
  local copies, waits for them, and re-layouts  53.5 us (7%)
  starting transfers between devices  50.7 us (7%)
  matrix products  37.1 us (5%)
  loops' own time  30.8 us (4%)
  between operations  15.7 us (2%)
  other arithmetic  9.27 us (1%)
    psum x2, waiting for transfers between devices, probe_update(): total_numer, total_denom = lax.psum((flat_numer, flat_denom), ('sy', 'sx'))  489 us
    another operation x2, loops' own time, local_terms(): lax.fori_loop(0, positions, place_patch, jnp.zeros((3,) + canvas.shape[1:...  30.4 us
    ppermute x8, starting transfers between devices, shifted(): lax.ppermute(value, axis, [(source, source + steps) for source in range(f...  26.3 us
    dynamic_update_slice x8, local copies, waits for them, and re-layouts, place_patch(): lax.dynamic_update_slice(running, existing + terms[number], (jnp.int32(0)...  22.4 us
    dot_general x16, matrix products, apply_right(): return jnp.einsum('bxy,yv->bxv', values, matrix, precision=HIGHEST)  19 us
    dot_general x16, matrix products, apply_left(): return jnp.einsum('ux,bxy->buy', matrix, values, precision=HIGHEST)  18.1 us
    gather x24, local copies, waits for them, and re-layouts  16.1 us
    ppermute x4, starting transfers between devices, extended(): lax.ppermute(lax.slice_in_dim(block, 0, width, axis=dim), axis, backward)  14.7 us
  transfers between devices with their start and end apart: 18, of which 11 were waited for; matrix products, arithmetic and copies ran while one was open for 1% of the time, Pallas kernels for 0%

commit v1 on v0

--- a/solution.py
+++ b/solution.py
@@ -121,7 +121,7 @@
     flat_numer = numerator.reshape(-1, extent * extent)
     flat_denom = denominator.reshape(extent * extent)
     flat_probe = probe_modes.reshape(-1, extent * extent)
-    total_numer, total_denom = lax.psum((flat_numer, flat_denom), ("sy", "sx"))
+    total_numer, total_denom = lax.psum(lax.psum((flat_numer, flat_denom), "sy"), "sx")
     updated = flat_probe - PROBE_STEP * total_numer / (total_denom[None] + REGULAR)
     return updated.reshape(probe_modes.shape)
 

time: 721 us -> 767 us (1.064)
  waiting for transfers between devices: 514 us -> 551 us
  starting transfers between devices: 50.7 us -> 58.4 us
    psum x2 -> x4, waiting for transfers between devices: 489 us -> 533 us  [the longest x2 272 us: probe_update(): lax.psum((flat_numer, flat_denom), 'sy')]
  transfers between devices with their start and end apart: 18 -> 20, of which waited for: 11 -> 14; matrix products, arithmetic and copies ran while one was open for 1% -> 2% of each run, Pallas kernels for 0% -> 0%
where the time goes in v1:
time: 767 us; the launch traced here: 756 us
  waiting for transfers between devices  551 us (72%)
  starting transfers between devices  58.4 us (8%)
  local copies, waits for them, and re-layouts  51.9 us (7%)
  matrix products  38.3 us (5%)
  loops' own time  31.1 us (4%)
  between operations  15.1 us (2%)
  other arithmetic  9.31 us (1%)
    psum x2, waiting for transfers between devices, probe_update(): lax.psum((flat_numer, flat_denom), 'sy')  272 us
    psum x2, waiting for transfers between devices, probe_update(): lax.psum(lax.psum((flat_numer, flat_denom), 'sy'), 'sx')  261 us
    another operation x2, loops' own time, local_terms(): lax.fori_loop(0, positions, place_patch, jnp.zeros((3,) + canvas.shape[1:...  30.7 us
    ppermute x8, starting transfers between devices, shifted(): lax.ppermute(value, axis, [(source, source + steps) for source in range(f...  28 us
    dynamic_update_slice x8, local copies, waits for them, and re-layouts, place_patch(): lax.dynamic_update_slice(running, existing + terms[number], (jnp.int32(0)...  22.4 us
    dot_general x16, matrix products, apply_right(): return jnp.einsum('bxy,yv->bxv', values, matrix, precision=HIGHEST)  19.9 us
    dot_general x16, matrix products, apply_left(): return jnp.einsum('ux,bxy->buy', matrix, values, precision=HIGHEST)  18.4 us
    ppermute x4, starting transfers between devices, extended(): lax.ppermute(lax.slice_in_dim(block, block.shape[dim] - width, None, axis...  16.1 us
  transfers between devices with their start and end apart: 20, of which 14 were waited for; matrix products, arithmetic and copies ran while one was open for 2% of the time, Pallas kernels for 0%

profile of v1, /device:TPU:8, one launch (start us, length us, event | category | flops | bytes accessed | tf_op | source)
XLA Modules:
  0.0 755.6 jit_solution(8374984833916894047)
XLA Ops:
  11.5 3.7 collective-permute-done.1
  15.4 3.8 collective-permute-start.2
  19.2 6.6 collective-permute-start.3
  30.1 8.3 %while.38 = (s32[]{:T(128)}, f32[2,256,256]{2,1,0:T(8,128)S(1)}, s32[4,3]{1,0:T(4,128)S(1)}, f32[4,2,128,128]{3,2,1,0:T(8,128)S(1)}, s32[]{:T(128)}) while((s32[]{:T(128)}, f32[2,256,256]{2,1,0:T(8,128)S(1)}, s32[4,3]{1,0:T(4,128)S(1)}, f32[4,2,128,128]{3,2,1,0:T(8,128)S(1)}, s32[]{:T(128)}) %tuple.147), condition=%wide.while_cond.8, body=%wide.while_body.8.sunk | while | flops 2 | bytes 262261 | solution.py:61
  58.2 29.6 %while.36 = (s32[]{:T(128)}, f32[3,256,256]{2,1,0:T(8,128)S(1)}, s32[4,2]{0,1:T(2,128)S(1)}, f32[4,3,128,128]{3,2,1,0:T(8,128)S(1)}, s32[]{:T(128)}, /*index=5*/s32[]{:T(128)}, s32[]{:T(128)}) while((s32[]{:T(128)}, f32[3,256,256]{2,1,0:T(8,128)S(1)}, s32[4,2]{0,1:T(2,128)S(1)}, f32[4,3,128,128]{3,2,1,0:T(8,128)S(1)}, s32[]{:T(128)}, ...), condition=%wide.region_5.6_spmd, body=%wide.region_4.5_spmd.sunk | while | flops 49160 | bytes 983237 | solution.py:113
  62.8 2.9 dynamic_update_slice.16
  70.3 2.8 dynamic_update_slice.16
  77.6 2.8 dynamic_update_slice.16
  87.9 5.8 collective-permute-start.4
  100.7 7.5 collective-permute-start.7
  112.6 6.7 collective-permute-start.8
  122.7 3.7 collective-permute-start.10
  126.4 4.9 collective-permute-start.11
  131.3 135.8 %all-reduce.15.cloned.1.call-done = (f32[4,16384]{1,0:T(4,128)}, f32[16384]{0:T(1024)}) async-done(((f32[4,16384]{1,0:T(4,128)}, f32[16384]{0:T(1024)}), (f32[4,16384]{1,0:T(4,128)}, f32[16384]{0:T(1024)})) %all-reduce.15.cloned.1.call-update) | async-done | bytes 327696 | tf_op jit(solution)/shard_map/psum | solution.py:124
  267.5 8.3 %while.39 = (s32[]{:T(128)}, f32[2,256,256]{2,1,0:T(8,128)S(1)}, s32[4,3]{1,0:T(4,128)S(1)}, f32[4,2,128,128]{3,2,1,0:T(8,128)S(1)}, s32[]{:T(128)}) while((s32[]{:T(128)}, f32[2,256,256]{2,1,0:T(8,128)S(1)}, s32[4,3]{1,0:T(4,128)S(1)}, f32[4,2,128,128]{3,2,1,0:T(8,128)S(1)}, s32[]{:T(128)}) %tuple.173), condition=%wide.while_cond.9, body=%wide.while_body.9.sunk | while | flops 2 | bytes 262261 | solution.py:61
  275.9 126.7 %all-reduce.11.cloned.1.call-done = (f32[4,16384]{1,0:T(4,128)}, f32[16384]{0:T(1024)}) async-done(((f32[4,16384]{1,0:T(4,128)}, f32[16384]{0:T(1024)}), (f32[4,16384]{1,0:T(4,128)}, f32[16384]{0:T(1024)})) %all-reduce.11.cloned.1.call-update) | async-done | bytes 327696 | tf_op jit(solution)/shard_map/psum | solution.py:124
  425.0 29.5 %while.37 = (s32[]{:T(128)}, f32[3,256,256]{2,1,0:T(8,128)S(1)}, s32[4,2]{0,1:T(2,128)S(1)}, f32[4,3,128,128]{3,2,1,0:T(8,128)S(1)}, s32[]{:T(128)}, /*index=5*/s32[]{:T(128)}, s32[]{:T(128)}) while((s32[]{:T(128)}, f32[3,256,256]{2,1,0:T(8,128)S(1)}, s32[4,2]{0,1:T(2,128)S(1)}, f32[4,3,128,128]{3,2,1,0:T(8,128)S(1)}, s32[]{:T(128)}, ...), condition=%wide.region_18.19_spmd, body=%wide.region_17.18_spmd.sunk | while | flops 49160 | bytes 983237 | solution.py:113
  429.6 2.9 dynamic_update_slice.17
  444.3 2.8 dynamic_update_slice.17
  458.2 3.0 collective-permute-done.13
  461.4 3.2 collective-permute-start.14
  465.7 4.8 collective-permute-start.15
  474.8 136.0 %all-reduce.13.cloned.1.call-done = (f32[4,16384]{1,0:T(4,128)}, f32[16384]{0:T(1024)}) async-done(((f32[4,16384]{1,0:T(4,128)}, f32[16384]{0:T(1024)}), (f32[4,16384]{1,0:T(4,128)}, f32[16384]{0:T(1024)})) %all-reduce.13.cloned.1.call-update) | async-done | bytes 327696 | tf_op jit(solution)/shard_map/psum | solution.py:124
  611.5 134.6 %all-reduce.9.cloned.1.call-done = (f32[4,16384]{1,0:T(4,128)}, f32[16384]{0:T(1024)}) async-done(((f32[4,16384]{1,0:T(4,128)}, f32[16384]{0:T(1024)}), (f32[4,16384]{1,0:T(4,128)}, f32[16384]{0:T(1024)})) %all-reduce.9.cloned.1.call-update) | async-done | bytes 327696 | tf_op jit(solution)/shard_map/psum | solution.py:124
  (213 shorter events, 108.5 us)
Async XLA Ops:
  7.2 259.9 %all-reduce.15.cloned.1.call-start = ((), (), s32[]{:S(2)}) async-start(), calls=%async_computation.3 | async-start | bytes 655360 | tf_op jit(solution)/shard_map/psum | solution.py:124
  8.1 3.3 collective-permute-start
  10.0 5.2 collective-permute-start.1
  15.4 12.9 %collective-permute-start.2 = (f32[2,256,64]{2,1,0:T(8,128)S(1)}, f32[2,256,64]{2,1,0:T(8,128)S(1)}, u32[]{:S(2)}, u32[]{:S(2)}) collective-permute-start(f32[2,256,64]{2,1,0:T(8,128)S(1)} %get-tuple-element.358), channel_id=1, source_target_pairs={{0,1},{1,2},{2,3},{3,4},{4,5},{5,6},{6,7},{7,8},{8,9},{9,10},{10,1... | collective-permute-start | bytes 393224 | tf_op jit(solution)/shard_map/ppermute | solution.py:18
  19.2 10.5 %collective-permute-start.3 = (f32[2,256,64]{2,1,0:T(8,128)S(1)}, f32[2,256,64]{2,1,0:T(8,128)S(1)}, u32[]{:S(2)}, u32[]{:S(2)}) collective-permute-start(f32[2,256,64]{2,1,0:T(8,128)S(1)} %get-tuple-element.359), channel_id=1, source_target_pairs={{1,0},{2,1},{3,2},{4,3},{5,4},{6,5},{7,6},{8,7},{9,8},{10,9},{11,1... | collective-permute-start | bytes 393224 | tf_op jit(solution)/shard_map/ppermute | solution.py:21
  87.9 7.4 collective-permute-start.4
  93.7 3.3 collective-permute-start.5
  97.2 11.9 %collective-permute-start.6 = (f32[3,128,64]{2,1,0:T(8,128)S(1)}, f32[3,128,64]{2,1,0:T(8,128)S(1)}, u32[]{:S(2)}, u32[]{:S(2)}) collective-permute-start(f32[3,128,64]{2,1,0:T(8,128)S(1)} %get-tuple-element.349), channel_id=1, source_target_pairs={{0,1},{1,2},{2,3},{3,4},{4,5},{5,6},{6,7},{7,8},{8,9},{9,10},{10,1... | collective-permute-start | bytes 294920 | tf_op jit(solution)/shard_map/ppermute | solution.py:29
  100.7 10.7 %collective-permute-start.7 = (f32[3,128,64]{2,1,0:T(8,128)S(1)}, f32[3,128,64]{2,1,0:T(8,128)S(1)}, u32[]{:S(2)}, u32[]{:S(2)}) collective-permute-start(f32[3,128,64]{2,1,0:T(8,128)S(1)} %get-tuple-element.348), channel_id=1, source_target_pairs={{1,0},{2,1},{3,2},{4,3},{5,4},{6,5},{7,6},{8,7},{9,8},{10,9},{11,1... | collective-permute-start | bytes 294920 | tf_op jit(solution)/shard_map/ppermute | solution.py:29
  112.6 9.0 %collective-permute-start.8 = (f32[2,64,128]{2,1,0:T(8,128)S(1)}, f32[2,64,128]{2,1,0:T(8,128)S(1)}, u32[]{:S(2)}, u32[]{:S(2)}) collective-permute-start(f32[2,64,128]{2,1,0:T(8,128)S(1)} %get-tuple-element.363), channel_id=1, source_target_pairs={{0,16},{16,32},{32,48},{48,64},{64,80},{80,96},{96,112},{112,128},... | collective-permute-start | bytes 196616 | tf_op jit(solution)/shard_map/ppermute | solution.py:18
  119.4 3.1 collective-permute-start.9
  121.6 281.0 %all-reduce.11.cloned.1.call-start = ((), (), s32[]{:S(2)}) async-start(), calls=%async_computation.1 | async-start | bytes 655360 | tf_op jit(solution)/shard_map/psum | solution.py:124
  122.7 144.5 %collective-permute-start.10 = (f32[2,256,64]{2,1,0:T(8,128)S(1)}, f32[2,256,64]{2,1,0:T(8,128)S(1)}, u32[]{:S(2)}, u32[]{:S(2)}) collective-permute-start(f32[2,256,64]{2,1,0:T(8,128)S(1)} %get-tuple-element.352), channel_id=1, source_target_pairs={{0,1},{1,2},{2,3},{3,4},{4,5},{5,6},{6,7},{7,8},{8,9},{9,10},{10,1... | collective-permute-start | bytes 393224 | tf_op jit(solution)/shard_map/ppermute | solution.py:18
  126.4 140.8 %collective-permute-start.11 = (f32[2,256,64]{2,1,0:T(8,128)S(1)}, f32[2,256,64]{2,1,0:T(8,128)S(1)}, u32[]{:S(2)}, u32[]{:S(2)}) collective-permute-start(f32[2,256,64]{2,1,0:T(8,128)S(1)} %get-tuple-element.353), channel_id=1, source_target_pairs={{1,0},{2,1},{3,2},{4,3},{5,4},{6,5},{7,6},{8,7},{9,8},{10,9},{11,1... | collective-permute-start | bytes 393224 | tf_op jit(solution)/shard_map/ppermute | solution.py:21
  267.1 343.7 %all-reduce.13.cloned.1.call-start = ((), (), s32[]{:S(2)}) async-start(), calls=%async_computation.2 | async-start | bytes 655360 | tf_op jit(solution)/shard_map/psum | solution.py:124
  275.8 129.5 %copy-start = (f32[4,128,128]{2,1,0:T(8,128)}, f32[4,128,128]{2,1,0:T(8,128)S(1)}, u32[]{:S(2)}) copy-start(f32[4,128,128]{2,1,0:T(8,128)S(1)} %slice_bitcast_fusion) | copy-start | bytes 786436
  275.8 127.6 %copy-start.12 = (f32[2,2,128,128]{3,2,1,0:T(8,128)S(1)}, f32[2,2,128,128]{3,2,1,0:T(8,128)}, u32[]{:S(2)}) copy-start(f32[2,2,128,128]{3,2,1,0:T(8,128)} %param.25) | copy-start | bytes 786436
  275.9 129.5 %copy-start.2 = (f32[4,128,128]{2,1,0:T(8,128)}, f32[4,128,128]{2,1,0:T(8,128)S(1)}, u32[]{:S(2)}) copy-start(f32[4,128,128]{2,1,0:T(8,128)S(1)} %slice_bitcast_fusion.2) | copy-start | bytes 786436
  454.5 3.7 collective-permute-start.12
  456.5 4.7 collective-permute-start.13
  461.4 10.5 %collective-permute-start.14 = (f32[3,128,64]{2,1,0:T(8,128)S(1)}, f32[3,128,64]{2,1,0:T(8,128)S(1)}, u32[]{:S(2)}, u32[]{:S(2)}) collective-permute-start(f32[3,128,64]{2,1,0:T(8,128)S(1)} %get-tuple-element.347), channel_id=1, source_target_pairs={{0,1},{1,2},{2,3},{3,4},{4,5},{5,6},{6,7},{7,8},{8,9},{9,10},{10,1... | collective-permute-start | bytes 294920 | tf_op jit(solution)/shard_map/ppermute | solution.py:29
  465.5 280.6 %all-reduce.9.cloned.1.call-start = ((), (), s32[]{:S(2)}) async-start(), calls=%async_computation | async-start | bytes 655360 | tf_op jit(solution)/shard_map/psum | solution.py:124
  465.7 7.9 %collective-permute-start.15 = (f32[3,128,64]{2,1,0:T(8,128)S(1)}, f32[3,128,64]{2,1,0:T(8,128)S(1)}, u32[]{:S(2)}, u32[]{:S(2)}) collective-permute-start(f32[3,128,64]{2,1,0:T(8,128)S(1)} %get-tuple-element.346), channel_id=1, source_target_pairs={{1,0},{2,1},{3,2},{4,3},{5,4},{6,5},{7,6},{8,7},{9,8},{10,9},{11,1... | collective-permute-start | bytes 294920 | tf_op jit(solution)/shard_map/ppermute | solution.py:29
  610.8 136.1 %copy-start.5 = (f32[4,16384]{1,0:T(4,128)S(1)}, f32[4,16384]{1,0:T(4,128)}, u32[]{:S(2)}) copy-start(f32[4,16384]{1,0:T(4,128)} %copy-done.4) | copy-start | bytes 786436
  (10 other events, 33.4 us)
Sparse Core Ops, SparseCore 0:
  121.7 145.3 all-reduce.14
  270.0 132.4 all-reduce.10
  465.6 145.1 all-reduce.12
  613.6 132.4 all-reduce.8
